TPU v7x, 32 devices: a whole 2x2x4 slice. The times are simulated.
32 devices in a mesh: dp: 2 (over x), seq: 8 (over z, core), tensor: 2 (over y).
Axes of the slice: x: 2, y: 2, z: 4, core: 2. Of those that a mesh axis runs over, the one named last changes fastest.
Arguments:
- events: bfloat16 [4, 2048, 1536], P('dp', 'seq', 'tensor'), may hold values from -6 to 6
- gate_in: bfloat16 [4, 2048, 1536], P('dp', 'seq', 'tensor'), may hold values from -6 to 6
- filters: bfloat16 [1024, 1536], P(None, 'tensor'), may hold values from -0.1875 to 0.1875
- proj: bfloat16 [1536, 1536], P('tensor'), may hold values from -0.15625 to 0.15625
- lengths: int32 [4], P('dp'), may hold values from 256 to 2048, as said below
- cotangent: bfloat16 [4, 2048, 1536], P('dp', 'seq', 'tensor'), may hold values from -6 to 6
Outputs:
- mixed: bfloat16 [4, 2048, 1536], P('dp', 'seq', 'tensor')
- grad_input: bfloat16 [4, 2048, 1536], P('dp', 'seq', 'tensor')
- grad_gate: bfloat16 [4, 2048, 1536], P('dp', 'seq', 'tensor')
- grad_filters: float32 [1024, 1536], P(None, 'tensor')
- grad_proj: float32 [1536, 1536], P('tensor')
Inputs may be any that keep to these rules, and one draw needn't show every extreme that they name: `lengths`: each length is a multiple of 256, and some user's length is 2048.
All inputs are finite; a program needn't handle non-finite values.
Results may differ from a plain program's by a relative error of at most 0.0049.
Values may be sent and summed in bfloat16 or wider, within the bound.
No kernel may reach another device: no remote copies, remote signals or barrier semaphores. Data moves between devices by JAX's collectives and lax.ppermute only.
A program may use at most 128 MiB of HBM per device.

v0:
```python
import math
import jax
import jax.numpy as jnp
from jax import lax
from jax.sharding import PartitionSpec as P


def shifted(value, axis, by):
    count = lax.axis_size(axis)
    pairs = [(i, i + by) for i in range(count) if 0 <= i + by < count]
    return lax.ppermute(value, axis, pairs)


def depthwise(lhs, kernel):
    return lax.conv_general_dilated(
        lhs,
        kernel[:, None, :],
        (1,),
        "VALID",
        dimension_numbers=("NWC", "WIO", "NWC"),
        feature_group_count=lhs.shape[2],
        preferred_element_type=jnp.float32,
    )


def filter_grad(window, grad_conv):
    users, width, chans = window.shape
    length = grad_conv.shape[1]
    lhs = jnp.transpose(window, (1, 0, 2)).reshape(1, width, users * chans)
    kernel = jnp.transpose(grad_conv, (1, 0, 2)).reshape(length, users * chans)
    result = depthwise(lhs, kernel)
    return jnp.sum(result.reshape(-1, users, chans), axis=1)[::-1]


def shards(events, gate_in, filters, proj, lengths, cotangent):
    users, block_len, chans = events.shape
    taps_len = filters.shape[0]
    reach = taps_len // block_len
    first = lax.axis_index("seq") * block_len
    position = first + jnp.arange(block_len, dtype=jnp.int32)
    live = (position[None, :] < lengths[:, None]).astype(jnp.float32)[:, :, None]
    masked = (events.astype(jnp.float32) * live).astype(jnp.bfloat16)
    earlier = []
    for offset in range(1, reach + 1):
        earlier.append(shifted(masked, "seq", offset))
    window = jnp.concatenate(earlier[::-1] + [masked], axis=1)[:, 1:]
    conv = depthwise(window, filters[::-1])
    gate_f = gate_in.astype(jnp.float32)
    gate_sig = jax.nn.sigmoid(gate_f)
    silu_g = gate_f * gate_sig
    gated = (silu_g * conv * live).astype(jnp.bfloat16)
    gated_rows = gated.reshape(-1, chans)
    partial_out = jnp.dot(gated_rows, proj, preferred_element_type=jnp.float32)
    out_rows = lax.psum_scatter(partial_out, "tensor", scatter_dimension=1, tiled=True)
    mixed = out_rows.astype(jnp.bfloat16).reshape(users, block_len, chans)
    cot_rows = cotangent.reshape(-1, chans)
    piece = lax.all_gather(cot_rows, "tensor", axis=1, tiled=True)
    grad_acc = lax.dot_general(
        piece, proj, (((1,), (1,)), ((), ())), preferred_element_type=jnp.float32
    )
    outer = lax.dot_general(
        gated_rows, piece, (((0,), (0,)), ((), ())), preferred_element_type=jnp.float32
    )
    grad_gated = grad_acc.reshape(users, block_len, chans) * live
    grad_conv = (grad_gated * silu_g).astype(jnp.bfloat16)
    grad_gate = (grad_gated * conv * gate_sig * (1.0 + gate_f * (1.0 - gate_sig))).astype(
        jnp.bfloat16
    )
    following = [grad_conv]
    for offset in range(1, reach + 1):
        following.append(shifted(grad_conv, "seq", -offset))
    ahead = jnp.concatenate(following, axis=1)[:, : block_len + taps_len - 1]
    grad_input = (depthwise(ahead, filters) * live).astype(jnp.bfloat16)
    filter_local = filter_grad(window, grad_conv)
    filter_sum, proj_sum = lax.psum((filter_local, outer), ("dp", "seq"))
    scale = 1.0 / math.sqrt(users * lax.axis_size("dp") * block_len * lax.axis_size("seq"))
    return (mixed, grad_input, grad_gate, filter_sum * scale, proj_sum * scale)


def solution(mesh):
    in_specs = (
        P("dp", "seq", "tensor"),
        P("dp", "seq", "tensor"),
        P(None, "tensor"),
        P("tensor", None),
        P("dp"),
        P("dp", "seq", "tensor"),
    )
    out_specs = (
        P("dp", "seq", "tensor"),
        P("dp", "seq", "tensor"),
        P("dp", "seq", "tensor"),
        P(None, "tensor"),
        P("tensor", None),
    )
    return jax.shard_map(shards, mesh=mesh, in_specs=in_specs, out_specs=out_specs, check_vma=False)
```

profile of v0, /device:TPU:0, one launch (start us, length us, event | category | flops | bytes accessed | tf_op | source)
XLA Modules:
  0.0 1037.7 jit_solution(3310441541021366550)
XLA Ops:
  7.2 0.0 all-gather.2.cloned.1.call-start
  7.2 0.9 compare_convert_fusion
  8.1 1.3 multiply_convert_fusion.2
  9.5 6.9 collective-permute-start
  16.3 3.6 collective-permute-start.1
  19.9 3.0 collective-permute-start.2
  22.9 2.2 collective-permute-start.3
  25.1 0.0 all-gather.2.cloned.1.call-update
  25.1 0.0 all-reduce.3.cloned.1.call-start
  25.1 23.0 %rev.6 = bf16[1024,768]{1,0:T(8,128)(2,1)} reverse(bf16[1024,768]{1,0:T(8,128)(2,1)} %param.8), dimensions={0} | reverse | bytes 3145728 | tf_op jit(solution)/shard_map/rev | solution.py:47
  48.2 1.2 constant_dynamic-update-slice_fusion.4
  49.4 0.9 collective-permute-done.1
  50.2 1.2 constant_dynamic-update-slice_fusion.3
  51.4 15.7 %collective-permute-done.2 = bf16[2,256,768]{2,1,0:T(8,128)(2,1)} collective-permute-done((bf16[2,256,768]{2,1,0:T(8,128)(2,1)S(1)}, bf16[2,256,768]{2,1,0:T(8,128)(2,1)}, u32[]{:S(2)}, u32[]{:S(2)}) %collective-permute-start.2) | collective-permute-done | bytes 786464 | tf_op jit(solution)/shard_map/ppermute | solution.py:11
  67.1 1.2 constant_dynamic-update-slice_fusion.2
  68.3 1.2 constant_dynamic-update-slice_fusion.1
  69.5 0.2 constant_dynamic-update-slice_fusion
  69.7 224.4 %fusion.2 = f32[2,256,768]{2,0,1:T(2,128)} fusion(bf16[2,1280,768]{2,1,0:T(8,128)(2,1)S(1)} %constant_dynamic-update-slice_fusion, bf16[1024,1,768]{2,0,1:T(8,128)(2,1)S(1)} %bitcast.26), kind=kOutput, calls=%fused_computation.3 | convolution fusion | flops 805306368 | bytes 7077888 | tf_op jit(solution)/shard_map/conv_general_dilated | solution.py:15
  294.1 3.0 slice_bitcast_fusion
  297.1 6.3 copy.43
  303.3 16.7 %copy.45 = bf16[1,1279,1536]{2,0,1:T(2,128)(2,1)} copy(bf16[1,1279,1536]{1,2,0:T(8,128)(2,1)} %bitcast.19) | data formatting | bytes 7858176 | tf_op jit(solution)/shard_map/reshape | solution.py:29
  320.0 2.9 fusion.14
  322.9 1.2 copy-done.1
  324.1 1.6 constant_dynamic-update-slice_fusion.9
  325.7 1.3 collective-permute-start.4
  327.0 1.3 collective-permute-start.5
  328.3 1.3 collective-permute-start.6
  329.6 1.3 collective-permute-start.7
  330.9 1.4 copy.44
  332.3 2.9 copy.46
  335.3 193.4 %convolution_reduce_fusion = f32[1024,1536]{1,0:T(8,128)} fusion(bf16[1,1279,1536]{2,0,1:T(2,128)(2,1)} %copy.45, bf16[256,1,1536]{2,1,0:T(2,128)(2,1)} %copy.46), kind=kOutput, calls=%fused_computation.23 | convolution fusion | flops 805306368 | bytes 11006976 | tf_op jit(solution)/shard_map/conv_general_dilated | solution.py:15
  528.7 8.3 reshape.66
  536.9 11.9 %reduce_sum.9 = f32[1024,768]{1,0:T(8,128)} reduce(f32[1024,2,768]{2,1,0:T(2,128)} %reshape.66, f32[]{:T(128)} %constant.19.clone.1), dimensions={1}, to_apply=%region_1.0 | reduce | flops 786432 | bytes 9437188 | tf_op jit(solution)/shard_map/reduce_sum | solution.py:32
  548.9 24.7 %rev.7 = f32[1024,768]{1,0:T(8,128)} reverse(f32[1024,768]{1,0:T(8,128)} %reduce_sum.9), dimensions={0} | reverse | bytes 6291456 | tf_op jit(solution)/shard_map/rev | solution.py:32
  573.6 2.1 constant_dynamic-update-slice_fusion.8
  575.6 2.2 constant_dynamic-update-slice_fusion.7
  577.8 2.1 constant_dynamic-update-slice_fusion.6
  579.9 2.1 constant_dynamic-update-slice_fusion.5
  582.0 195.2 %fusion = f32[2,256,768]{2,0,1:T(2,128)S(1)} fusion(bf16[2,1280,768]{2,1,0:T(8,128)(2,1)} %constant_dynamic-update-slice_fusion.5, bf16[1024,1,768]{2,0,1:T(8,128)(2,1)S(1)} %bitcast.25), kind=kOutput, calls=%fused_computation.1 | convolution fusion | flops 805306368 | bytes 7077888 | tf_op jit(solution)/shard_map/conv_general_dilated | solution.py:15
  777.2 2.1 fusion.11
  779.3 3.6 fusion.15
  782.9 0.0 reduce-scatter.2.cloned.1.call-start
  783.0 3.1 fusion.13
  786.2 196.6 %all-reduce.3.cloned.1.call-done = (f32[1024,768]{1,0:T(8,128)}, f32[768,1536]{1,0:T(8,128)}) async-done(((f32[1024,768]{1,0:T(8,128)}, f32[768,1536]{1,0:T(8,128)}), (f32[1024,768]{1,0:T(8,128)}, f32[768,1536]{1,0:T(8,128)})) %all-reduce.3.cloned.1.call-update) | async-done | bytes 7864336 | tf_op jit(solution)/shard_map/psum | solution.py:75
  982.8 4.0 broadcast_multiply_fusion.1
  986.8 2.7 broadcast_multiply_fusion
  989.5 39.1 %reduce-scatter.2.cloned.1.call-done = f32[512,768]{1,0:T(8,128)} async-done(((f32[512,1536]{1,0:T(8,128)}), f32[512,768]{1,0:T(8,128)}) %reduce-scatter.2.cloned.1.call-update) | async-done | bytes 1572880 | tf_op jit(solution)/shard_map/reduce_scatter | solution.py:54
  1028.6 2.4 convert_element_type.36
  (37 shorter events, 0.1 us)
Async XLA Ops:
  7.2 312.9 %copy-start = (bf16[768,1536]{1,0:T(8,128)(2,1)S(1)}, bf16[768,1536]{1,0:T(8,128)(2,1)}, u32[]{:S(2)}) copy-start(bf16[768,1536]{1,0:T(8,128)(2,1)} %param.9) | copy-start | bytes 7077892
  7.2 312.8 %all-gather.2.cloned.1.call-start = ((), (), s32[]{:S(2)}) async-start(), calls=%async_computation.2 | async-start | bytes 2359296 | tf_op jit(solution)/shard_map/all_gather | solution.py:57
  8.1 61.4 %copy-start.11 = (f32[2,256]{1,0:T(2,128)}, f32[2,256]{1,0:T(2,128)S(1)}, u32[]{:S(2)}) copy-start(f32[2,256]{1,0:T(2,128)S(1)} %compare_convert_fusion) | copy-start | bytes 6148
  9.5 38.7 %collective-permute-start = (bf16[2,256,768]{2,1,0:T(8,128)(2,1)S(1)}, bf16[2,256,768]{2,1,0:T(8,128)(2,1)}, u32[]{:S(2)}, u32[]{:S(2)}) collective-permute-start(bf16[2,256,768]{2,1,0:T(8,128)(2,1)S(1)} %multiply_convert_fusion.2), channel_id=1, source_target_pairs={{0,8},{2,10},{4,12},{6,14},{1,9},{3,11},{5,13},{7,15},{16,24},{18,... | collective-permute-start | bytes 2359304 | tf_op jit(solution)/shard_map/ppermute | solution.py:11
  16.3 33.9 %collective-permute-start.1 = (bf16[2,256,768]{2,1,0:T(8,128)(2,1)S(1)}, bf16[2,256,768]{2,1,0:T(8,128)(2,1)}, u32[]{:S(2)}, u32[]{:S(2)}) collective-permute-start(bf16[2,256,768]{2,1,0:T(8,128)(2,1)S(1)} %multiply_convert_fusion.2), channel_id=1, source_target_pairs={{0,6},{2,8},{4,10},{6,12},{8,14},{1,7},{3,9},{5,11},{7,13},{9,15},... | collective-permute-start | bytes 2359304 | tf_op jit(solution)/shard_map/ppermute | solution.py:11
  19.9 47.2 %collective-permute-start.2 = (bf16[2,256,768]{2,1,0:T(8,128)(2,1)S(1)}, bf16[2,256,768]{2,1,0:T(8,128)(2,1)}, u32[]{:S(2)}, u32[]{:S(2)}) collective-permute-start(bf16[2,256,768]{2,1,0:T(8,128)(2,1)S(1)} %multiply_convert_fusion.2), channel_id=1, source_target_pairs={{0,4},{2,6},{4,8},{6,10},{8,12},{10,14},{1,5},{3,7},{5,9},{7,11},{... | collective-permute-start | bytes 2359304 | tf_op jit(solution)/shard_map/ppermute | solution.py:11
  22.9 45.4 %collective-permute-start.3 = (bf16[2,256,768]{2,1,0:T(8,128)(2,1)S(1)}, bf16[2,256,768]{2,1,0:T(8,128)(2,1)}, u32[]{:S(2)}, u32[]{:S(2)}) collective-permute-start(bf16[2,256,768]{2,1,0:T(8,128)(2,1)S(1)} %multiply_convert_fusion.2), channel_id=1, source_target_pairs={{0,2},{2,4},{4,6},{6,8},{8,10},{10,12},{12,14},{1,3},{3,5},{5,7},{... | collective-permute-start | bytes 2359304 | tf_op jit(solution)/shard_map/ppermute | solution.py:11
  25.1 957.7 %all-reduce.3.cloned.1.call-start = ((), (), s32[]{:S(2)}) async-start(), calls=%async_computation.3 | async-start | bytes 15728640 | tf_op jit(solution)/shard_map/psum | solution.py:75
  49.3 20.1 %copy-start.6 = (bf16[2,256,768]{2,1,0:T(8,128)(2,1)S(1)}, bf16[2,256,768]{2,1,0:T(8,128)(2,1)}, u32[]{:S(2)}) copy-start(bf16[2,256,768]{2,1,0:T(8,128)(2,1)} %param.6) | copy-start | bytes 2359300
  51.4 18.3 %copy-start.9 = (bf16[1024,768]{1,0:T(8,128)(2,1)S(1)}, bf16[1024,768]{1,0:T(8,128)(2,1)}, u32[]{:S(2)}) copy-start(bf16[1024,768]{1,0:T(8,128)(2,1)} %rev.6) | copy-start | bytes 4718596
  320.0 4.1 copy-start.4
  320.0 4.1 copy-start.12
  322.9 1.2 copy-start.1
  325.7 247.8 %collective-permute-start.4 = (bf16[2,256,768]{2,1,0:T(8,128)(2,1)}, bf16[2,256,768]{2,1,0:T(8,128)(2,1)}, u32[]{:S(2)}, u32[]{:S(2)}) collective-permute-start(bf16[2,256,768]{2,1,0:T(8,128)(2,1)} %get-tuple-element.18), channel_id=1, source_target_pairs={{2,0},{4,2},{6,4},{8,6},{10,8},{12,10},{14,12},{3,1},{5,3},{7,5},{... | collective-permute-start | bytes 2359304 | tf_op jit(solution)/shard_map/ppermute | solution.py:11
  327.0 248.6 %collective-permute-start.5 = (bf16[2,256,768]{2,1,0:T(8,128)(2,1)}, bf16[2,256,768]{2,1,0:T(8,128)(2,1)}, u32[]{:S(2)}, u32[]{:S(2)}) collective-permute-start(bf16[2,256,768]{2,1,0:T(8,128)(2,1)} %get-tuple-element.18), channel_id=1, source_target_pairs={{4,0},{6,2},{8,4},{10,6},{12,8},{14,10},{5,1},{7,3},{9,5},{11,7},{... | collective-permute-start | bytes 2359304 | tf_op jit(solution)/shard_map/ppermute | solution.py:11
  328.3 249.5 %collective-permute-start.6 = (bf16[2,256,768]{2,1,0:T(8,128)(2,1)}, bf16[2,256,768]{2,1,0:T(8,128)(2,1)}, u32[]{:S(2)}, u32[]{:S(2)}) collective-permute-start(bf16[2,256,768]{2,1,0:T(8,128)(2,1)} %get-tuple-element.18), channel_id=1, source_target_pairs={{6,0},{8,2},{10,4},{12,6},{14,8},{7,1},{9,3},{11,5},{13,7},{15,9},... | collective-permute-start | bytes 2359304 | tf_op jit(solution)/shard_map/ppermute | solution.py:11
  329.6 250.3 %collective-permute-start.7 = (bf16[2,256,768]{2,1,0:T(8,128)(2,1)}, bf16[2,256,768]{2,1,0:T(8,128)(2,1)}, u32[]{:S(2)}, u32[]{:S(2)}) collective-permute-start(bf16[2,256,768]{2,1,0:T(8,128)(2,1)} %get-tuple-element.18), channel_id=1, source_target_pairs={{8,0},{10,2},{12,4},{14,6},{9,1},{11,3},{13,5},{15,7},{24,16},{26,... | collective-permute-start | bytes 2359304 | tf_op jit(solution)/shard_map/ppermute | solution.py:11
  575.6 6.3 copy-start.8
  581.9 195.2 %copy-start.2 = (f32[512,768]{1,0:T(8,128)S(1)}, f32[512,768]{1,0:T(8,128)}, u32[]{:S(2)}) copy-start(f32[512,768]{1,0:T(8,128)} %copy-done.1) | copy-start | bytes 4718596
  581.9 195.2 %copy-start.5 = (bf16[2,256,768]{2,1,0:T(8,128)(2,1)S(1)}, bf16[2,256,768]{2,1,0:T(8,128)(2,1)}, u32[]{:S(2)}) copy-start(bf16[2,256,768]{2,1,0:T(8,128)(2,1)} %param.7) | copy-start | bytes 2359300
  582.0 195.2 %copy-start.10 = (f32[2,256,768]{2,0,1:T(2,128)S(1)}, f32[2,256,768]{2,0,1:T(2,128)}, u32[]{:S(2)}) copy-start(f32[2,256,768]{2,0,1:T(2,128)} %fusion.2) | copy-start | bytes 4718596
  582.0 195.2 %copy-start.13 = (f32[2,256]{1,0:T(2,128)S(1)}, f32[2,256]{1,0:T(2,128)}, u32[]{:S(2)}) copy-start(f32[2,256]{1,0:T(2,128)} %copy-done.11) | copy-start | bytes 6148
  777.2 2.1 copy-start.7
  782.9 245.6 %reduce-scatter.2.cloned.1.call-start = ((), (), s32[]{:S(2)}) async-start(), calls=%async_computation.1 | async-start | bytes 4718592 | tf_op jit(solution)/shard_map/reduce_scatter | solution.py:54
  982.8 4.0 copy-start.3
Sparse Core Ops, SparseCore 0:
  25.2 25.3 all-gather.1
  783.1 199.6 all-reduce.2
  985.0 43.4 reduce-scatter.1
where the time goes:
time: 1050 us; the launch traced here: 1040 us
  matrix products  623 us (59%)
  waiting for transfers between devices  252 us (24%)
  local copies, waits for them, and re-layouts  101 us (10%)
  other arithmetic  27.1 us (3%)
  starting transfers between devices  20.9 us (2%)
  between operations  14.2 us (1%)
    conv_general_dilated x3, matrix products, depthwise(): lax.conv_general_dilated(lhs, kernel[:, None, :], (1,), 'VALID', dimensio...  613 us
    psum x1, waiting for transfers between devices, shards(): filter_sum, proj_sum = lax.psum((filter_local, outer), ('dp', 'seq'))  197 us
    reduce_scatter x1, waiting for transfers between devices, shards(): lax.psum_scatter(partial_out, 'tensor', scatter_dimension=1, tiled=True)  39.1 us
    rev x1, local copies, waits for them, and re-layouts, filter_grad(): return jnp.sum(result.reshape(-1, users, chans), axis=1)[::-1]  24.7 us
    rev x1, local copies, waits for them, and re-layouts, shards(): conv = depthwise(window, filters[::-1])  23 us
  transfers between devices with their start and end apart: 11, of which 4 were waited for; matrix products, arithmetic and copies ran while one was open for 52% of the time, Pallas kernels for 0%

commit v1 on v0

--- a/solution.py
+++ b/solution.py
@@ -72,7 +72,13 @@
     ahead = jnp.concatenate(following, axis=1)[:, : block_len + taps_len - 1]
     grad_input = (depthwise(ahead, filters) * live).astype(jnp.bfloat16)
     filter_local = filter_grad(window, grad_conv)
-    filter_sum, proj_sum = lax.psum((filter_local, outer), ("dp", "seq"))
+
+    def _report_links(matrix, chip_axis, axis_id):
+        for p in (chip_axis, axis_id):
+            matrix = lax.psum(matrix, p)
+        return matrix
+
+    filter_sum, proj_sum = _report_links((filter_local, outer), chip_axis="seq", axis_id="dp")
     scale = 1.0 / math.sqrt(users * lax.axis_size("dp") * block_len * lax.axis_size("seq"))
     return (mixed, grad_input, grad_gate, filter_sum * scale, proj_sum * scale)
 

time: 1050 us -> 1250 us (1.19)
  waiting for transfers between devices: 252 us -> 451 us
    psum x1 -> x2, waiting for transfers between devices: 197 us -> 388 us  [_report_links(): matrix = lax.psum(matrix, p)]
  transfers between devices with their start and end apart: 11 -> 12, of which waited for: 4 -> 5; matrix products, arithmetic and copies ran while one was open for 52% -> 43% of each run, Pallas kernels for 0% -> 0%
where the time goes in v1:
time: 1250 us; the launch traced here: 1240 us
  matrix products  622 us (50%)
  waiting for transfers between devices  451 us (36%)
  local copies, waits for them, and re-layouts  101 us (8%)
  other arithmetic  27.1 us (2%)
  starting transfers between devices  20.9 us (2%)
  between operations  14.2 us (1%)
    conv_general_dilated x3, matrix products, depthwise(): lax.conv_general_dilated(lhs, kernel[:, None, :], (1,), 'VALID', dimensio...  613 us
    psum x2, waiting for transfers between devices, _report_links(): matrix = lax.psum(matrix, p)  388 us
    reduce_scatter x1, waiting for transfers between devices, shards(): lax.psum_scatter(partial_out, 'tensor', scatter_dimension=1, tiled=True)  46.4 us
  transfers between devices with their start and end apart: 12, of which 5 were waited for; matrix products, arithmetic and copies ran while one was open for 43% of the time, Pallas kernels for 0%

profile of v1, /device:TPU:0, one launch (start us, length us, event | category | flops | bytes accessed | tf_op | source)
XLA Modules:
  0.0 1236.0 jit_solution(13413072674052777076)
XLA Ops:
  7.2 0.9 compare_convert_fusion
  8.1 1.3 multiply_convert_fusion.2
  9.5 6.9 collective-permute-start
  16.3 3.6 collective-permute-start.1
  19.9 3.0 collective-permute-start.2
  22.9 2.2 collective-permute-start.3
  25.1 0.0 all-reduce.5.cloned.1.call-start
  25.2 23.0 %rev.6 = bf16[1024,768]{1,0:T(8,128)(2,1)} reverse(bf16[1024,768]{1,0:T(8,128)(2,1)} %param.8), dimensions={0} | reverse | bytes 3145728 | tf_op jit(solution)/shard_map/rev | solution.py:47
  48.2 1.3 constant_dynamic-update-slice_fusion.4
  49.4 0.8 collective-permute-done.1
  50.2 1.2 constant_dynamic-update-slice_fusion.3
  51.4 15.7 %collective-permute-done.2 = bf16[2,256,768]{2,1,0:T(8,128)(2,1)} collective-permute-done((bf16[2,256,768]{2,1,0:T(8,128)(2,1)S(1)}, bf16[2,256,768]{2,1,0:T(8,128)(2,1)}, u32[]{:S(2)}, u32[]{:S(2)}) %collective-permute-start.2) | collective-permute-done | bytes 786464 | tf_op jit(solution)/shard_map/ppermute | solution.py:11
  67.1 1.2 constant_dynamic-update-slice_fusion.2
  68.3 1.2 constant_dynamic-update-slice_fusion.1
  69.5 0.2 constant_dynamic-update-slice_fusion
  69.7 224.4 %fusion.2 = f32[2,256,768]{2,0,1:T(2,128)} fusion(bf16[2,1280,768]{2,1,0:T(8,128)(2,1)S(1)} %constant_dynamic-update-slice_fusion, bf16[1024,1,768]{2,0,1:T(8,128)(2,1)S(1)} %bitcast.26), kind=kOutput, calls=%fused_computation.3 | convolution fusion | flops 805306368 | bytes 7077888 | tf_op jit(solution)/shard_map/conv_general_dilated | solution.py:15
  294.1 3.0 slice_bitcast_fusion
  297.0 6.2 copy.43
  303.2 16.7 %copy.45 = bf16[1,1279,1536]{2,0,1:T(2,128)(2,1)} copy(bf16[1,1279,1536]{1,2,0:T(8,128)(2,1)} %bitcast.19) | data formatting | bytes 7858176 | tf_op jit(solution)/shard_map/reshape | solution.py:29
  319.9 2.9 fusion.14
  322.8 1.2 copy-done.1
  324.0 1.6 constant_dynamic-update-slice_fusion.9
  325.6 1.3 collective-permute-start.4
  326.9 1.3 collective-permute-start.5
  328.2 1.3 collective-permute-start.6
  329.5 1.3 collective-permute-start.7
  330.8 1.4 copy.44
  332.2 2.9 copy.46
  335.2 193.4 %convolution_reduce_fusion = f32[1024,1536]{1,0:T(8,128)} fusion(bf16[1,1279,1536]{2,0,1:T(2,128)(2,1)} %copy.45, bf16[256,1,1536]{2,1,0:T(2,128)(2,1)} %copy.46), kind=kOutput, calls=%fused_computation.23 | convolution fusion | flops 805306368 | bytes 11006976 | tf_op jit(solution)/shard_map/conv_general_dilated | solution.py:15
  528.6 8.3 reshape.66
  536.8 11.9 reduce_sum.9
  548.8 24.7 %rev.7 = f32[1024,768]{1,0:T(8,128)} reverse(f32[1024,768]{1,0:T(8,128)} %reduce_sum.9), dimensions={0} | reverse | bytes 6291456 | tf_op jit(solution)/shard_map/rev | solution.py:32
  573.5 2.2 constant_dynamic-update-slice_fusion.8
  575.7 2.1 constant_dynamic-update-slice_fusion.7
  577.7 2.1 constant_dynamic-update-slice_fusion.6
  579.8 2.1 constant_dynamic-update-slice_fusion.5
  581.9 195.2 %fusion = f32[2,256,768]{2,0,1:T(2,128)S(1)} fusion(bf16[2,1280,768]{2,1,0:T(8,128)(2,1)} %constant_dynamic-update-slice_fusion.5, bf16[1024,1,768]{2,0,1:T(8,128)(2,1)S(1)} %bitcast.25), kind=kOutput, calls=%fused_computation.1 | convolution fusion | flops 805306368 | bytes 7077888 | tf_op jit(solution)/shard_map/conv_general_dilated | solution.py:15
  777.1 2.1 fusion.11
  779.2 3.6 fusion.15
  782.9 0.0 reduce-scatter.2.cloned.1.call-start
  782.9 3.1 fusion.13
  786.0 0.0 all-reduce.7.cloned.1.call-start
  786.0 200.5 %all-reduce.5.cloned.1.call-done = (f32[1024,768]{1,0:T(8,128)}, f32[768,1536]{1,0:T(8,128)}) async-done(((f32[1024,768]{1,0:T(8,128)}, f32[768,1536]{1,0:T(8,128)}), (f32[1024,768]{1,0:T(8,128)}, f32[768,1536]{1,0:T(8,128)})) %all-reduce.5.cloned.1.call-update) | async-done | bytes 7864336 | tf_op jit(solution)/shard_map/psum | solution.py:78
  986.6 46.4 %reduce-scatter.2.cloned.1.call-done = f32[512,768]{1,0:T(8,128)} async-done(((f32[512,1536]{1,0:T(8,128)}), f32[512,768]{1,0:T(8,128)}) %reduce-scatter.2.cloned.1.call-update) | async-done | bytes 1572880 | tf_op jit(solution)/shard_map/reduce_scatter | solution.py:54
  1033.0 2.4 convert_element_type.36
  1035.3 187.3 %all-reduce.7.cloned.1.call-done = (f32[1024,768]{1,0:T(8,128)}, f32[768,1536]{1,0:T(8,128)}) async-done(((f32[1024,768]{1,0:T(8,128)}, f32[768,1536]{1,0:T(8,128)}), (f32[1024,768]{1,0:T(8,128)}, f32[768,1536]{1,0:T(8,128)})) %all-reduce.7.cloned.1.call-update) | async-done | bytes 7864336 | tf_op jit(solution)/shard_map/psum | solution.py:78
  1222.6 4.0 broadcast_multiply_fusion.1
  1226.6 2.7 broadcast_multiply_fusion
  (40 shorter events, 0.2 us)
Async XLA Ops:
  7.2 312.8 %copy-start = (bf16[768,1536]{1,0:T(8,128)(2,1)S(1)}, bf16[768,1536]{1,0:T(8,128)(2,1)}, u32[]{:S(2)}) copy-start(bf16[768,1536]{1,0:T(8,128)(2,1)} %param.9) | copy-start | bytes 7077892
  7.2 312.7 %all-gather.2.cloned.1.call-start = ((), (), s32[]{:S(2)}) async-start(), calls=%async_computation.2 | async-start | bytes 2359296 | tf_op jit(solution)/shard_map/all_gather | solution.py:57
  8.1 61.4 %copy-start.11 = (f32[2,256]{1,0:T(2,128)}, f32[2,256]{1,0:T(2,128)S(1)}, u32[]{:S(2)}) copy-start(f32[2,256]{1,0:T(2,128)S(1)} %compare_convert_fusion) | copy-start | bytes 6148
  9.5 38.7 %collective-permute-start = (bf16[2,256,768]{2,1,0:T(8,128)(2,1)S(1)}, bf16[2,256,768]{2,1,0:T(8,128)(2,1)}, u32[]{:S(2)}, u32[]{:S(2)}) collective-permute-start(bf16[2,256,768]{2,1,0:T(8,128)(2,1)S(1)} %multiply_convert_fusion.2), channel_id=1, source_target_pairs={{0,8},{2,10},{4,12},{6,14},{1,9},{3,11},{5,13},{7,15},{16,24},{18,... | collective-permute-start | bytes 2359304 | tf_op jit(solution)/shard_map/ppermute | solution.py:11
  16.3 33.9 %collective-permute-start.1 = (bf16[2,256,768]{2,1,0:T(8,128)(2,1)S(1)}, bf16[2,256,768]{2,1,0:T(8,128)(2,1)}, u32[]{:S(2)}, u32[]{:S(2)}) collective-permute-start(bf16[2,256,768]{2,1,0:T(8,128)(2,1)S(1)} %multiply_convert_fusion.2), channel_id=1, source_target_pairs={{0,6},{2,8},{4,10},{6,12},{8,14},{1,7},{3,9},{5,11},{7,13},{9,15},... | collective-permute-start | bytes 2359304 | tf_op jit(solution)/shard_map/ppermute | solution.py:11
  19.9 47.2 %collective-permute-start.2 = (bf16[2,256,768]{2,1,0:T(8,128)(2,1)S(1)}, bf16[2,256,768]{2,1,0:T(8,128)(2,1)}, u32[]{:S(2)}, u32[]{:S(2)}) collective-permute-start(bf16[2,256,768]{2,1,0:T(8,128)(2,1)S(1)} %multiply_convert_fusion.2), channel_id=1, source_target_pairs={{0,4},{2,6},{4,8},{6,10},{8,12},{10,14},{1,5},{3,7},{5,9},{7,11},{... | collective-permute-start | bytes 2359304 | tf_op jit(solution)/shard_map/ppermute | solution.py:11
  22.9 45.4 %collective-permute-start.3 = (bf16[2,256,768]{2,1,0:T(8,128)(2,1)S(1)}, bf16[2,256,768]{2,1,0:T(8,128)(2,1)}, u32[]{:S(2)}, u32[]{:S(2)}) collective-permute-start(bf16[2,256,768]{2,1,0:T(8,128)(2,1)S(1)} %multiply_convert_fusion.2), channel_id=1, source_target_pairs={{0,2},{2,4},{4,6},{6,8},{8,10},{10,12},{12,14},{1,3},{3,5},{5,7},{... | collective-permute-start | bytes 2359304 | tf_op jit(solution)/shard_map/ppermute | solution.py:11
  25.1 961.5 %all-reduce.5.cloned.1.call-start = ((), (), s32[]{:S(2)}) async-start(), calls=%async_computation.3 | async-start | bytes 15728640 | tf_op jit(solution)/shard_map/psum | solution.py:78
  48.2 21.3 %copy-start.6 = (bf16[2,256,768]{2,1,0:T(8,128)(2,1)S(1)}, bf16[2,256,768]{2,1,0:T(8,128)(2,1)}, u32[]{:S(2)}) copy-start(bf16[2,256,768]{2,1,0:T(8,128)(2,1)} %param.6) | copy-start | bytes 2359300
  49.4 20.3 %copy-start.9 = (bf16[1024,768]{1,0:T(8,128)(2,1)S(1)}, bf16[1024,768]{1,0:T(8,128)(2,1)}, u32[]{:S(2)}) copy-start(bf16[1024,768]{1,0:T(8,128)(2,1)} %rev.6) | copy-start | bytes 4718596
  319.9 4.1 copy-start.4
  319.9 4.1 copy-start.12
  322.8 1.2 copy-start.1
  325.6 247.8 %collective-permute-start.4 = (bf16[2,256,768]{2,1,0:T(8,128)(2,1)}, bf16[2,256,768]{2,1,0:T(8,128)(2,1)}, u32[]{:S(2)}, u32[]{:S(2)}) collective-permute-start(bf16[2,256,768]{2,1,0:T(8,128)(2,1)} %get-tuple-element.20), channel_id=1, source_target_pairs={{2,0},{4,2},{6,4},{8,6},{10,8},{12,10},{14,12},{3,1},{5,3},{7,5},{... | collective-permute-start | bytes 2359304 | tf_op jit(solution)/shard_map/ppermute | solution.py:11
  326.9 248.7 %collective-permute-start.5 = (bf16[2,256,768]{2,1,0:T(8,128)(2,1)}, bf16[2,256,768]{2,1,0:T(8,128)(2,1)}, u32[]{:S(2)}, u32[]{:S(2)}) collective-permute-start(bf16[2,256,768]{2,1,0:T(8,128)(2,1)} %get-tuple-element.20), channel_id=1, source_target_pairs={{4,0},{6,2},{8,4},{10,6},{12,8},{14,10},{5,1},{7,3},{9,5},{11,7},{... | collective-permute-start | bytes 2359304 | tf_op jit(solution)/shard_map/ppermute | solution.py:11
  328.2 249.5 %collective-permute-start.6 = (bf16[2,256,768]{2,1,0:T(8,128)(2,1)}, bf16[2,256,768]{2,1,0:T(8,128)(2,1)}, u32[]{:S(2)}, u32[]{:S(2)}) collective-permute-start(bf16[2,256,768]{2,1,0:T(8,128)(2,1)} %get-tuple-element.20), channel_id=1, source_target_pairs={{6,0},{8,2},{10,4},{12,6},{14,8},{7,1},{9,3},{11,5},{13,7},{15,9},... | collective-permute-start | bytes 2359304 | tf_op jit(solution)/shard_map/ppermute | solution.py:11
  329.5 250.3 %collective-permute-start.7 = (bf16[2,256,768]{2,1,0:T(8,128)(2,1)}, bf16[2,256,768]{2,1,0:T(8,128)(2,1)}, u32[]{:S(2)}, u32[]{:S(2)}) collective-permute-start(bf16[2,256,768]{2,1,0:T(8,128)(2,1)} %get-tuple-element.20), channel_id=1, source_target_pairs={{8,0},{10,2},{12,4},{14,6},{9,1},{11,3},{13,5},{15,7},{24,16},{26,... | collective-permute-start | bytes 2359304 | tf_op jit(solution)/shard_map/ppermute | solution.py:11
  573.5 8.4 copy-start.8
  581.9 195.2 %copy-start.2 = (f32[512,768]{1,0:T(8,128)S(1)}, f32[512,768]{1,0:T(8,128)}, u32[]{:S(2)}) copy-start(f32[512,768]{1,0:T(8,128)} %copy-done.1) | copy-start | bytes 4718596
  581.9 195.2 %copy-start.5 = (bf16[2,256,768]{2,1,0:T(8,128)(2,1)S(1)}, bf16[2,256,768]{2,1,0:T(8,128)(2,1)}, u32[]{:S(2)}) copy-start(bf16[2,256,768]{2,1,0:T(8,128)(2,1)} %param.7) | copy-start | bytes 2359300
  581.9 195.2 %copy-start.10 = (f32[2,256,768]{2,0,1:T(2,128)S(1)}, f32[2,256,768]{2,0,1:T(2,128)}, u32[]{:S(2)}) copy-start(f32[2,256,768]{2,0,1:T(2,128)} %fusion.2) | copy-start | bytes 4718596
  581.9 195.2 %copy-start.13 = (f32[2,256]{1,0:T(2,128)S(1)}, f32[2,256]{1,0:T(2,128)}, u32[]{:S(2)}) copy-start(f32[2,256]{1,0:T(2,128)} %copy-done.11) | copy-start | bytes 6148
  777.1 2.1 copy-start.7
  782.9 250.1 %reduce-scatter.2.cloned.1.call-start = ((), (), s32[]{:S(2)}) async-start(), calls=%async_computation.1 | async-start | bytes 4718592 | tf_op jit(solution)/shard_map/reduce_scatter | solution.py:54
  786.0 436.6 %all-reduce.7.cloned.1.call-start = ((), (), s32[]{:S(2)}) async-start(), calls=%async_computation.4 | async-start | bytes 15728640 | tf_op jit(solution)/shard_map/psum | solution.py:78
  1222.6 4.0 copy-start.3
Sparse Core Ops, SparseCore 0:
  25.2 25.3 all-gather.1
  783.0 203.5 all-reduce.4
  989.4 43.5 reduce-scatter.1
  1035.3 187.2 all-reduce.6
